TPU v7x, 32 devices: a whole 2x2x4 slice. The times are simulated.
32 devices in a mesh: parts: 2 (over y), slab: 4 (over z), orb: 2 (over x), pen: 2 (over core).
Axes of the slice: x: 2, y: 2, z: 4, core: 2. Of those that a mesh axis runs over, the one named last changes fastest.
Arguments:
- orbitals: float32 [128, 16, 8, 256], P(('parts', 'orb'), 'slab', 'pen'), parts along dimension 0, may hold values from -7.6 to 7.6
- energies: float32 [128], P(('parts', 'orb')), parts along dimension 0, may hold values from -1 to 0.5
- frequency: float32 [2], P('parts'), parts along dimension 0, may hold values from 0.5 to 2
- local_potential: float32 [16, 8, 256], P('slab', 'pen'), may hold values from -1 to 1
- perturbation: float32 [16, 8, 256], P('slab', 'pen'), may hold values from 0.5 to 1.5
- projectors: float32 [128, 8, 256], P(None, 'pen'), may hold values from -0.0625 to 0.0625
- profiles: float32 [128, 5], replicated, may hold values from 0.5 to 2
- couplings: float32 [128], replicated, may hold values from 4 to 12
- atom_planes: int32 [128], replicated, may hold values from 0 to 15
Outputs:
- response_real: float32 [128, 16, 8, 256], P(('parts', 'orb'), 'slab', 'pen'), parts along dimension 0
- density: float32 [32, 8, 256], P(('parts', 'slab'), 'pen'), parts along dimension 0
There are 2 independent parts, one for each index of `parts`. A program takes and returns all parts, laid end to end along the dimension named above; an argument that names none is the same for every part. Nothing has to cross between parts.
Inputs may be any that keep to these rules, and one draw needn't show every extreme that they name: Projector a covers the planes (atom_planes[a] + d) mod 16 of the first dimension for d < 5.
All inputs are finite; a program needn't handle non-finite values.
Results may differ from a plain program's by a relative error of at most 0.0003.
Values sent between devices are 32-bit elements; how exact they have to be, the bound alone decides.
A program may use at most 64 MiB of HBM per device.

v0:
```python
import jax
import jax.numpy as jnp
from jax import lax
from jax.sharding import PartitionSpec as P

NOCC = 64
ITERS = 2


kinetic_scale = 0.125
highest = lax.Precision.HIGHEST


def extended(cells, sides, width):
    for axis, dim in sides:
        count = lax.axis_size(axis)
        head = lax.slice_in_dim(cells, 0, width, axis=dim)
        tail = lax.slice_in_dim(cells, cells.shape[dim] - width, cells.shape[dim], axis=dim)
        cells = jnp.concatenate(
            [
                lax.ppermute(tail, axis, [(i, (i + 1) % count) for i in range(count)]),
                cells,
                lax.ppermute(head, axis, [((i + 1) % count, i) for i in range(count)]),
            ],
            axis=dim,
        )
    return cells


def plane_weights(atom_planes, profiles, planes, depth_total):
    span_size = profiles.shape[1]
    covered = (atom_planes[:, None] + jnp.arange(span_size, dtype=jnp.int32)[None, :]) % depth_total
    matches = (covered[:, :, None] == planes[None, None, :]).astype(jnp.float32)
    return jnp.sum(profiles[:, :, None] * matches, axis=1)


def coefficients(values, projectors, weights, couplings):
    orb_count, plane_count, row_count, col_count = values.shape
    flat_values = values.reshape(orb_count * plane_count, row_count * col_count)
    flat_beta = projectors.reshape(projectors.shape[0], row_count * col_count)
    inner_sums = lax.dot_general(
        flat_beta, flat_values, (((1,), (1,)), ((), ())), precision=highest
    )
    inner_sums = inner_sums.reshape(projectors.shape[0], orb_count, plane_count)
    partial_sum = jnp.einsum("aiz,az->ai", inner_sums, weights, precision=highest)
    summed = lax.psum(partial_sum, ("slab", "pen"))
    return couplings[:, None] * summed


def apply_section(padded, potential, beta_out, weights_out, expansion, energies):
    centre = padded[:, 1:-1, 1:-1]
    beside_all = (
        padded[:, 2:, 1:-1] + padded[:, :-2, 1:-1] + padded[:, 1:-1, 2:] + padded[:, 1:-1, :-2]
    )
    beside_all = beside_all + jnp.roll(centre, 1, 3) + jnp.roll(centre, -1, 3)
    orb_count, plane_count, row_count, col_count = centre.shape
    spread = weights_out[:, None, :] * expansion[:, :, None]
    flat_spread = spread.reshape(spread.shape[0], orb_count * plane_count)
    flat_beta = beta_out.reshape(beta_out.shape[0], row_count * col_count)
    nonlocal_term = lax.dot_general(
        flat_spread, flat_beta, (((0,), (0,)), ((), ())), precision=highest
    )
    nonlocal_term = nonlocal_term.reshape(orb_count, plane_count, row_count, col_count)
    return (
        kinetic_scale * (6.0 * centre - beside_all)
        + potential[None] * centre
        + nonlocal_term
        - energies[:, None, None, None] * centre
    )


def on_device(
    orbitals,
    energies,
    frequency,
    local_potential,
    perturbation,
    projectors,
    profiles,
    couplings,
    atom_planes,
):
    orb_count, plane_count, row_count, col_count = orbitals.shape
    depth_total = plane_count * lax.axis_size("slab")
    cell_total = float(depth_total * row_count * lax.axis_size("pen") * col_count)
    first_plane = lax.axis_index("slab") * plane_count
    planes = (first_plane + jnp.arange(plane_count, dtype=jnp.int32)) % depth_total
    weights = plane_weights(atom_planes, profiles, planes, depth_total)
    freq_square = frequency[0] * frequency[0]
    everyone = lax.all_gather(orbitals, "orb", axis=0, tiled=True)
    every_flat = everyone.reshape(everyone.shape[0], -1)

    def correlation_terms(values):
        return lax.dot_general(
            every_flat, values.reshape(orb_count, -1), (((1,), (1,)), ((), ())), precision=highest
        )

    def removed(values, totals, factor):
        expansion = jax.scipy.linalg.cho_solve((factor, True), totals / cell_total)
        removed_part = lax.dot_general(
            expansion, every_flat, (((0,), (0,)), ((), ())), precision=highest
        )
        return values - removed_part.reshape(values.shape)

    def squares(values):
        return lax.psum(jnp.sum(values * values, axis=(1, 2, 3)), ("slab", "pen"))

    def apply_shallow(values):
        padded = extended(values, (("slab", 1), ("pen", 2)), 1)
        expansion = coefficients(values, projectors, weights, couplings)
        return apply_section(padded, local_potential, projectors, weights, expansion, energies)

    source = perturbation[None] * orbitals
    gram_part = lax.dot_general(every_flat, every_flat, (((1,), (1,)), ((), ())), precision=highest)
    gram_total, source_total = lax.psum((gram_part, correlation_terms(source)), ("slab", "pen"))
    factor = jnp.linalg.cholesky(gram_total / cell_total)
    residual = -removed(source, source_total, factor)
    direction = residual
    solution = jnp.zeros_like(residual)
    norm_now = squares(residual)
    for iteration in range(ITERS):
        direction_total = lax.psum(correlation_terms(direction), ("slab", "pen"))
        inner_field = removed(direction, direction_total, factor)
        first_half = apply_shallow(inner_field)
        second = apply_shallow(first_half)
        first_half, second = (first_half, second)
        target = second + freq_square * inner_field
        curve_part = jnp.sum(first_half * first_half, axis=(1, 2, 3)) + freq_square * jnp.sum(
            inner_field * inner_field, axis=(1, 2, 3)
        )
        image_total, curvature = lax.psum((correlation_terms(target), curve_part), ("slab", "pen"))
        image_field = removed(target, image_total, factor)
        step_size = norm_now / curvature
        solution = solution + step_size[:, None, None, None] * direction
        residual = residual - step_size[:, None, None, None] * image_field
        norm_next = squares(residual)
        direction = residual + (norm_next / norm_now)[:, None, None, None] * direction
        norm_now = norm_next
    padded = extended(solution, (("slab", 1), ("pen", 2)), 1)
    final_expansion = coefficients(solution, projectors, weights, couplings)
    response_real = apply_section(
        padded, local_potential, projectors, weights, final_expansion, energies
    )
    density = lax.psum(jnp.sum(orbitals * response_real, axis=0), "orb") * (4.0 / NOCC)
    return (response_real, density)


def solution(mesh):
    in_specs = (
        P(("parts", "orb"), "slab", "pen", None),
        P(("parts", "orb")),
        P("parts"),
        P("slab", "pen", None),
        P("slab", "pen", None),
        P(None, "pen", None),
        P(),
        P(),
        P(),
    )
    out_specs = (P(("parts", "orb"), "slab", "pen", None), P(("parts", "slab"), "pen", None))
    return jax.shard_map(
        on_device, mesh=mesh, in_specs=in_specs, out_specs=out_specs, check_vma=False
    )
```

profile of v0, /device:TPU:0, one launch (start us, length us, event | category | flops | bytes accessed | tf_op | source)
XLA Modules:
  0.0 372.5 jit_solution(15849839324657514728)
XLA Ops:
  7.2 2.1 copy.40
  12.3 21.8 %all-gather.2.cloned.1.call-done = f32[64,4,4,256]{3,0,2,1:T(8,128)} async-done(((f32[32,4,4,256]{3,0,2,1:T(8,128)}), f32[64,4,4,256]{3,0,2,1:T(8,128)}) %all-gather.2.cloned.1.call-update) | async-done | bytes 1048592 | tf_op jit(solution)/shard_map/all_gather | solution.py:90
  34.1 2.6 convolution_bitcast_fusion
  37.9 28.8 %all-reduce.1 = (f32[64,64]{0,1:T(8,128)S(1)}, f32[64,32]{0,1:T(8,128)S(1)}) all-reduce(f32[64,64]{0,1:T(8,128)S(1)} %convolution_bitcast_fusion, f32[64,32]{0,1:T(8,128)S(1)} %convolution_bitcast_fusion.4), channel_id=1, replica_groups=mesh['parts'=2,'slab'=4,'orb'=2,'pen'=2] {'slab','pen'}, use_global_device_ids=true, to_apply=%region_0.1 | all-reduce | flops 6144 | bytes 49152 | tf_op jit(solution)/shard_map/psum | solution.py:115
  66.8 5.8 %cholesky.18 = f32[64,64]{1,0:T(8,128)S(1)} custom-call(f32[64,64]{1,0:T(8,128)S(1)} %fusion.65), custom_call_target="Cholesky" | custom-call | tf_op jit(solution)/shard_map/jit(cholesky)/cholesky | solution.py:116
  74.0 4.9 %custom-call.11 = f32[1,64,64]{1,2,0:T(8,128)S(1)} custom-call(f32[1,64,64]{2,1,0:T(8,128)S(1)} %fusion.52), custom_call_target="InvertDiagBlocksLowerTriangular" | custom-call | tf_op jit(solution)/shard_map/jit(_cho_solve)/triangular_solve | solution.py:99
  85.9 25.9 %psum.101 = f32[64,32]{0,1:T(8,128)S(1)} all-reduce(f32[64,32]{0,1:T(8,128)S(1)} %convolution_bitcast_fusion.3), channel_id=1, replica_groups=mesh['parts'=2,'slab'=4,'orb'=2,'pen'=2] {'slab','pen'}, use_global_device_ids=true, to_apply=%region_6.8 | all-reduce | flops 2048 | bytes 16384 | tf_op jit(solution)/shard_map/psum | solution.py:122
  116.6 3.8 %collective-permute-start = (f32[32,1,4,256]{3,0,2,1:T(8,128)}, f32[32,1,4,256]{3,0,2,1:T(8,128)}, u32[]{:S(2)}, u32[]{:S(2)}) collective-permute-start(f32[32,1,4,256]{3,0,2,1:T(8,128)} %get-tuple-element.45), channel_id=1, source_target_pairs={{4,0},{8,4},{12,8},{0,12},{5,1},{9,5},{13,9},{1,13},{6,2},{10,6},{... | collective-permute-start | bytes 393224 | tf_op jit(solution)/shard_map/ppermute | solution.py:23
  122.1 25.9 %psum.102 = f32[128,32]{0,1:T(8,128)S(1)} all-reduce(f32[128,32]{0,1:T(8,128)S(1)} %multiply_reduce_fusion.9), channel_id=1, replica_groups=mesh['parts'=2,'slab'=4,'orb'=2,'pen'=2] {'slab','pen'}, use_global_device_ids=true, to_apply=%region_8.10 | all-reduce | flops 4096 | bytes 32768 | tf_op jit(solution)/shard_map/psum | solution.py:46
  151.5 2.2 multiply_reduce_fusion.4
  156.8 3.8 %collective-permute-start.4 = (f32[32,1,4,256]{3,0,2,1:T(8,128)}, f32[32,1,4,256]{3,0,2,1:T(8,128)}, u32[]{:S(2)}, u32[]{:S(2)}) collective-permute-start(f32[32,1,4,256]{3,0,2,1:T(8,128)} %get-tuple-element.39), channel_id=1, source_target_pairs={{4,0},{8,4},{12,8},{0,12},{5,1},{9,5},{13,9},{1,13},{6,2},{10,6},{... | collective-permute-start | bytes 393224 | tf_op jit(solution)/shard_map/ppermute | solution.py:23
  162.3 25.9 %psum.104 = f32[128,32]{0,1:T(8,128)S(1)} all-reduce(f32[128,32]{0,1:T(8,128)S(1)} %multiply_reduce_fusion.8), channel_id=1, replica_groups=mesh['parts'=2,'slab'=4,'orb'=2,'pen'=2] {'slab','pen'}, use_global_device_ids=true, to_apply=%region_12.14 | all-reduce | flops 4096 | bytes 32768 | tf_op jit(solution)/shard_map/psum | solution.py:46
  191.2 2.3 fusion.6
  194.5 26.0 %all-reduce = (f32[64,32]{0,1:T(8,128)S(1)}, f32[32]{0:T(128)S(1)}, f32[32]{0:T(128)S(1)}) all-reduce(f32[64,32]{0,1:T(8,128)S(1)} %convolution_bitcast_fusion.2, f32[32]{0:T(128)S(1)} %get-tuple-element.46, f32[32]{0:T(128)S(1)} %multiply_add_fusion.3), channel_id=1, replica_groups=mesh['parts'=2,'slab'=4,'orb'=2,'pen'=2] {'slab','pen'}, use_global_device_ids=true, to_apply=%region_13.15 | all-reduce | flops 2112 | bytes 16896 | tf_op jit(solution)/shard_map/psum | solution.py:131
  220.9 2.5 multiply_reduce_fusion.2
  223.3 13.6 %psum.106 = f32[32]{0:T(128)S(1)} all-reduce(f32[32]{0:T(128)S(1)} %get-tuple-element.52), channel_id=1, replica_groups=mesh['parts'=2,'slab'=4,'orb'=2,'pen'=2] {'slab','pen'}, use_global_device_ids=true, to_apply=%region_15.17 | all-reduce | flops 32 | bytes 256 | tf_op jit(solution)/shard_map/psum | solution.py:106
  237.9 25.9 %psum.107 = f32[64,32]{0,1:T(8,128)S(1)} all-reduce(f32[64,32]{0,1:T(8,128)S(1)} %convolution_bitcast_fusion.1), channel_id=1, replica_groups=mesh['parts'=2,'slab'=4,'orb'=2,'pen'=2] {'slab','pen'}, use_global_device_ids=true, to_apply=%region_16.18 | all-reduce | flops 2048 | bytes 16384 | tf_op jit(solution)/shard_map/psum | solution.py:122
  268.6 3.8 %collective-permute-start.8 = (f32[32,1,4,256]{3,0,2,1:T(8,128)}, f32[32,1,4,256]{3,0,2,1:T(8,128)}, u32[]{:S(2)}, u32[]{:S(2)}) collective-permute-start(f32[32,1,4,256]{3,0,2,1:T(8,128)} %get-tuple-element.33), channel_id=1, source_target_pairs={{4,0},{8,4},{12,8},{0,12},{5,1},{9,5},{13,9},{1,13},{6,2},{10,6},{... | collective-permute-start | bytes 393224 | tf_op jit(solution)/shard_map/ppermute | solution.py:23
  274.1 26.1 %psum.108 = f32[128,32]{0,1:T(8,128)S(1)} all-reduce(f32[128,32]{0,1:T(8,128)S(1)} %multiply_reduce_fusion.7), channel_id=1, replica_groups=mesh['parts'=2,'slab'=4,'orb'=2,'pen'=2] {'slab','pen'}, use_global_device_ids=true, to_apply=%region_17.19 | all-reduce | flops 4096 | bytes 32768 | tf_op jit(solution)/shard_map/psum | solution.py:46
  303.0 2.2 fusion.8
  305.2 13.8 %psum.109 = f32[32]{0:T(128)S(1)} all-reduce(f32[32]{0:T(128)S(1)} %multiply_add_fusion.2), channel_id=1, replica_groups=mesh['parts'=2,'slab'=4,'orb'=2,'pen'=2] {'slab','pen'}, use_global_device_ids=true, to_apply=%region_20.22 | all-reduce | flops 32 | bytes 256 | tf_op jit(solution)/shard_map/psum | solution.py:131
  321.4 3.8 %collective-permute-start.12 = (f32[32,1,4,256]{3,0,2,1:T(8,128)}, f32[32,1,4,256]{3,0,2,1:T(8,128)}, u32[]{:S(2)}, u32[]{:S(2)}) collective-permute-start(f32[32,1,4,256]{3,0,2,1:T(8,128)} %get-tuple-element.27), channel_id=1, source_target_pairs={{4,0},{8,4},{12,8},{0,12},{5,1},{9,5},{13,9},{1,13},{6,2},{10,6},{... | collective-permute-start | bytes 393224 | tf_op jit(solution)/shard_map/ppermute | solution.py:23
  326.0 25.9 %psum.110 = f32[128,32]{0,1:T(8,128)S(1)} all-reduce(f32[128,32]{0,1:T(8,128)S(1)} %multiply_reduce_fusion.6), channel_id=1, replica_groups=mesh['parts'=2,'slab'=4,'orb'=2,'pen'=2] {'slab','pen'}, use_global_device_ids=true, to_apply=%region_21.23 | all-reduce | flops 4096 | bytes 32768 | tf_op jit(solution)/shard_map/psum | solution.py:46
  356.7 7.2 %psum.111 = f32[4,4,256]{2,1,0:T(4,128)S(1)} all-reduce(f32[4,4,256]{2,1,0:T(4,128)S(1)} %get-tuple-element.56), channel_id=1, replica_groups=mesh['parts'=2,'slab'=4,'orb'=2,'pen'=2] {'orb'}, use_global_device_ids=true, to_apply=%region_23.25 | all-reduce | flops 4096 | bytes 32768 | tf_op jit(solution)/shard_map/psum | solution.py:144
  (156 shorter events, 50.4 us)
Async XLA Ops:
  7.2 27.0 %all-gather.2.cloned.1.call-start = ((), (), s32[]{:S(2)}) async-start(), calls=%async_computation | async-start | bytes 1572864 | tf_op jit(solution)/shard_map/all_gather | solution.py:90
  12.3 24.4 %copy-start.7 = (f32[32,4,4,256]{3,2,1,0:T(4,128)S(1)}, f32[32,4,4,256]{3,2,1,0:T(4,128)}, u32[]{:S(2)}) copy-start(f32[32,4,4,256]{3,2,1,0:T(4,128)} %param.11) | copy-start | bytes 1572868
  12.3 24.4 %copy-start.18 = (f32[4,4,256]{2,1,0:T(4,128)S(1)}, f32[4,4,256]{2,1,0:T(4,128)}, u32[]{:S(2)}) copy-start(f32[4,4,256]{2,1,0:T(4,128)} %param.15) | copy-start | bytes 49156
  116.6 31.5 %collective-permute-start.1 = (f32[32,1,4,256]{3,0,2,1:T(8,128)}, f32[32,1,4,256]{3,0,2,1:T(8,128)}, u32[]{:S(2)}, u32[]{:S(2)}) collective-permute-start(f32[32,1,4,256]{3,0,2,1:T(8,128)} %get-tuple-element.44), channel_id=1, source_target_pairs={{0,4},{4,8},{8,12},{12,0},{1,5},{5,9},{9,13},{13,1},{2,6},{6,10},{... | collective-permute-start | bytes 393224 | tf_op jit(solution)/shard_map/ppermute | solution.py:21
  116.6 31.5 %collective-permute-start = (f32[32,1,4,256]{3,0,2,1:T(8,128)}, f32[32,1,4,256]{3,0,2,1:T(8,128)}, u32[]{:S(2)}, u32[]{:S(2)}) collective-permute-start(f32[32,1,4,256]{3,0,2,1:T(8,128)} %get-tuple-element.45), channel_id=1, source_target_pairs={{4,0},{8,4},{12,8},{0,12},{5,1},{9,5},{13,9},{1,13},{6,2},{10,6},{... | collective-permute-start | bytes 393224 | tf_op jit(solution)/shard_map/ppermute | solution.py:23
  122.1 25.9 %copy-start.19 = (f32[128]{0:T(128)S(1)}, f32[128]{0:T(128)}, u32[]{:S(2)}) copy-start(f32[128]{0:T(128)} %param.18) | copy-start | bytes 1540
  148.1 2.8 copy-start.11
  149.0 1.5 collective-permute-start.2
  149.1 1.7 collective-permute-start.3
  156.8 31.5 %collective-permute-start.5 = (f32[32,1,4,256]{3,0,2,1:T(8,128)}, f32[32,1,4,256]{3,0,2,1:T(8,128)}, u32[]{:S(2)}, u32[]{:S(2)}) collective-permute-start(f32[32,1,4,256]{3,0,2,1:T(8,128)} %get-tuple-element.38), channel_id=1, source_target_pairs={{0,4},{4,8},{8,12},{12,0},{1,5},{5,9},{9,13},{13,1},{2,6},{6,10},{... | collective-permute-start | bytes 393224 | tf_op jit(solution)/shard_map/ppermute | solution.py:21
  156.8 31.5 %collective-permute-start.4 = (f32[32,1,4,256]{3,0,2,1:T(8,128)}, f32[32,1,4,256]{3,0,2,1:T(8,128)}, u32[]{:S(2)}, u32[]{:S(2)}) collective-permute-start(f32[32,1,4,256]{3,0,2,1:T(8,128)} %get-tuple-element.39), channel_id=1, source_target_pairs={{4,0},{8,4},{12,8},{0,12},{5,1},{9,5},{13,9},{1,13},{6,2},{10,6},{... | collective-permute-start | bytes 393224 | tf_op jit(solution)/shard_map/ppermute | solution.py:23
  188.2 3.0 copy-start.16
  188.2 3.0 copy-start.6
  188.2 3.0 copy-start.12
  189.4 1.5 collective-permute-start.6
  189.5 1.7 collective-permute-start.7
  268.6 31.6 %collective-permute-start.9 = (f32[32,1,4,256]{3,0,2,1:T(8,128)}, f32[32,1,4,256]{3,0,2,1:T(8,128)}, u32[]{:S(2)}, u32[]{:S(2)}) collective-permute-start(f32[32,1,4,256]{3,0,2,1:T(8,128)} %get-tuple-element.32), channel_id=1, source_target_pairs={{0,4},{4,8},{8,12},{12,0},{1,5},{5,9},{9,13},{13,1},{2,6},{6,10},{... | collective-permute-start | bytes 393224 | tf_op jit(solution)/shard_map/ppermute | solution.py:21
  268.6 31.7 %collective-permute-start.8 = (f32[32,1,4,256]{3,0,2,1:T(8,128)}, f32[32,1,4,256]{3,0,2,1:T(8,128)}, u32[]{:S(2)}, u32[]{:S(2)}) collective-permute-start(f32[32,1,4,256]{3,0,2,1:T(8,128)} %get-tuple-element.33), channel_id=1, source_target_pairs={{4,0},{8,4},{12,8},{0,12},{5,1},{9,5},{13,9},{1,13},{6,2},{10,6},{... | collective-permute-start | bytes 393224 | tf_op jit(solution)/shard_map/ppermute | solution.py:23
  301.2 1.5 collective-permute-start.10
  301.3 1.7 collective-permute-start.11
  321.4 30.5 %collective-permute-start.13 = (f32[32,1,4,256]{3,0,2,1:T(8,128)}, f32[32,1,4,256]{3,0,2,1:T(8,128)}, u32[]{:S(2)}, u32[]{:S(2)}) collective-permute-start(f32[32,1,4,256]{3,0,2,1:T(8,128)} %get-tuple-element.26), channel_id=1, source_target_pairs={{0,4},{4,8},{8,12},{12,0},{1,5},{5,9},{9,13},{13,1},{2,6},{6,10},{... | collective-permute-start | bytes 393224 | tf_op jit(solution)/shard_map/ppermute | solution.py:21
  321.4 30.5 %collective-permute-start.12 = (f32[32,1,4,256]{3,0,2,1:T(8,128)}, f32[32,1,4,256]{3,0,2,1:T(8,128)}, u32[]{:S(2)}, u32[]{:S(2)}) collective-permute-start(f32[32,1,4,256]{3,0,2,1:T(8,128)} %get-tuple-element.27), channel_id=1, source_target_pairs={{4,0},{8,4},{12,8},{0,12},{5,1},{9,5},{13,9},{1,13},{6,2},{10,6},{... | collective-permute-start | bytes 393224 | tf_op jit(solution)/shard_map/ppermute | solution.py:23
  352.8 1.5 collective-permute-start.14
  352.9 1.7 collective-permute-start.15
  (17 other events, 28.6 us)
Sparse Core Ops, SparseCore 0:
  10.1 23.9 all-gather.1
where the time goes:
time: 373 us; the launch traced here: 372 us
  blocking collectives  245 us (66%)
  waiting for transfers between devices  26.6 us (7%)
  matrix products  25.8 us (7%)
  local copies, waits for them, and re-layouts  24.9 us (7%)
  starting transfers between devices  17.6 us (5%)
  other arithmetic  17.1 us (5%)
  between operations  15.3 us (4%)
    psum x4, blocking collectives, coefficients(): summed = lax.psum(partial_sum, ('slab', 'pen'))  104 us
    psum x2, blocking collectives, on_device(): direction_total = lax.psum(correlation_terms(direction), ('slab', 'pen'))  51.8 us
    psum x2, blocking collectives, on_device(): lax.psum((correlation_terms(target), curve_part), ('slab', 'pen'))  39.8 us
    psum x1, blocking collectives, on_device(): lax.psum((gram_part, correlation_terms(source)), ('slab', 'pen'))  28.8 us
    all_gather x1, waiting for transfers between devices, on_device(): everyone = lax.all_gather(orbitals, 'orb', axis=0, tiled=True)  21.8 us
    ppermute x8, starting transfers between devices, extended(): lax.ppermute(head, axis, [((i + 1) % count, i) for i in range(count)])  15.6 us
    psum x1, blocking collectives, squares(): return lax.psum(jnp.sum(values * values, axis=(1, 2, 3)), ('slab', 'pen'))  13.6 us
    dot_general x4, matrix products, apply_section(): lax.dot_general(flat_spread, flat_beta, (((0,), (0,)), ((), ())), precisi...  8.76 us
  transfers between devices with their start and end apart: 17, of which 9 were waited for; matrix products, arithmetic and copies ran while one was open for 1% of the time, Pallas kernels for 0%

commit v1 on v0

v1 whole, which is shorter than its diff:
```python
import functools

import jax
import jax.numpy as jnp
from jax import lax
from jax.experimental import pallas as pl
from jax.experimental.pallas import tpu as pltpu
from jax.sharding import PartitionSpec as P

kinetic_scale = 0.125
MESH = pl.DeviceIdType.MESH
f32, bf16 = jnp.float32, jnp.bfloat16
NT = (((1,), (1,)), ((), ()))
NN = (((1,), (0,)), ((), ()))


def split(x):
    hi = x.astype(bf16)
    return hi, (x - hi.astype(f32)).astype(bf16)


def dot3(a, b, dims):
    rows = a[0].shape[0]
    both = lax.dot_general(jnp.concatenate(a, axis=0), b[0], dims, preferred_element_type=f32)
    rest = lax.dot_general(a[0], b[1], dims, preferred_element_type=f32)
    return both[:rows] + both[rows:] + rest


def inverse(a):
    size = a.shape[0]
    row_id = lax.broadcasted_iota(jnp.int32, (size, size), 0)
    col_id = lax.broadcasted_iota(jnp.int32, (size, size), 1)
    one_row = lax.broadcasted_iota(jnp.int32, (1, size), 1)
    for k in range(size):
        inv = 1.0 / a[k : k + 1, k : k + 1]
        column = a[:, k : k + 1]
        row = jnp.where(one_row == k, inv, a[k : k + 1, :] * inv)
        updated = jnp.where(col_id == k, 0.0, a) - column * row
        a = jnp.where(row_id == k, row, updated)
    return a


def kernel(
    slabs, pens, orbs, orb_ref, en_ref, freq_ref, vloc_ref, dv_ref, beta_ref, table_ref, coup_ref,
    resp_ref, dens_ref,
    others, phi_hi, phi_lo, u_hi, u_lo, pad0, pad1, pad2, work, dens_slots,
    gram_slots, red_slots,
    gather_send, gather_recv, halo_send, halo_recv, red_send, red_recv, dens_send, dens_recv,
):
    planes, rows, count, width = orb_ref.shape
    atoms = beta_ref.shape[1]
    span = table_ref.shape[1] - 1
    total_orbs = count * orbs
    depth = planes * slabs
    cells = float(depth * rows * pens * width)
    slab, pen, orb = lax.axis_index("slab"), lax.axis_index("pen"), lax.axis_index("orb")
    group = slabs * pens
    me = slab * pens + pen

    def peer(k):
        target = lax.rem(me + k, group)
        return {"slab": target // pens, "pen": lax.rem(target, pens)}

    barrier = pltpu.get_barrier_semaphore()
    for k in range(1, group):
        pl.semaphore_signal(barrier, inc=1, device_id=peer(k), device_id_type=MESH)
    for k in range(1, orbs):
        pl.semaphore_signal(
            barrier, inc=1, device_id={"orb": lax.rem(orb + k, orbs)}, device_id_type=MESH
        )
    pl.semaphore_wait(barrier, group - 1 + orbs - 1)

    sent = []

    def start(src, dst, send, recv, device):
        copy = pltpu.make_async_remote_copy(
            src_ref=src, dst_ref=dst, send_sem=send, recv_sem=recv,
            device_id=device, device_id_type=MESH,
        )
        copy.start()
        sent.append(copy)
        return copy

    gathers = [
        start(orb_ref, others.at[k - 1], gather_send.at[k - 1], gather_recv.at[k - 1],
              {"orb": lax.rem(orb + k, orbs)})
        for k in range(1, orbs)
    ]

    def halo_start(pad, index):
        up, down = lax.rem(slab + 1, slabs), lax.rem(slab + slabs - 1, slabs)
        right, left = lax.rem(pen + 1, pens), lax.rem(pen + pens - 1, pens)
        inner_p, inner_r = pl.ds(1, planes), pl.ds(1, rows)
        sides = (
            (pad.at[planes, inner_r], pad.at[0, inner_r], {"slab": up}),
            (pad.at[1, inner_r], pad.at[planes + 1, inner_r], {"slab": down}),
            (pad.at[inner_p, rows], pad.at[inner_p, 0], {"pen": right}),
            (pad.at[inner_p, 1], pad.at[inner_p, rows + 1], {"pen": left}),
        )
        return [
            start(src, dst, halo_send.at[index, side], halo_recv.at[index, side], device)
            for side, (src, dst, device) in enumerate(sides)
        ]

    def reduce_start(slots, index, values):
        slots[me] = values
        return [
            start(slots.at[me], slots.at[me], red_send.at[index, k - 1], red_recv.at[index, k - 1],
                  peer(k))
            for k in range(1, group)
        ]

    def reduce_end(slots, copies, index):
        for k in range(1, group):
            source = lax.rem(me + group - k, group)
            pltpu.make_async_remote_copy(
                src_ref=slots.at[source], dst_ref=slots.at[source],
                send_sem=red_send.at[index, k - 1], recv_sem=red_recv.at[index, k - 1],
                device_id=peer(k), device_id_type=MESH,
            ).wait_recv()
        total = slots[0]
        for k in range(1, group):
            total = total + slots[k]
        return total

    atom = table_ref[:, span : span + 1]
    for z in range(planes):
        plane = (slab * planes + z).astype(f32)
        weight = jnp.zeros((atoms, 1), f32)
        for d in range(span):
            covered = atom + float(d)
            covered = jnp.where(covered >= float(depth), covered - float(depth), covered)
            weight = weight + jnp.where(covered == plane, table_ref[:, d : d + 1], 0.0)
        for y in range(rows):
            hi, lo = split(beta_ref[y] * weight)
            u_hi[z, y] = hi
            u_lo[z, y] = lo

    for copy in gathers:
        copy.wait_recv()

    def put_phi(z, carry):
        for y in range(rows):
            for k in range(orbs):
                hi, lo = split(orb_ref[z, y] if k == 0 else others[k - 1, z, y])
                phi_hi[z, y, k * count : (k + 1) * count] = hi
                phi_lo[z, y, k * count : (k + 1) * count] = lo
        return carry

    lax.fori_loop(0, planes, put_phi, 0)

    def phi(z, y):
        return phi_hi[z, y], phi_lo[z, y]

    def u(z, y):
        return u_hi[z, y], u_lo[z, y]

    def gram_part(z, acc):
        for y in range(rows):
            source = dv_ref[z, pl.ds(y, 1), :] * orb_ref[z, y]
            s_hi, s_lo = split(source)
            left = (
                jnp.concatenate([phi_hi[z, y], s_hi], axis=0),
                jnp.concatenate([phi_lo[z, y], s_lo], axis=0),
            )
            acc = acc + dot3(left, phi(z, y), NT)
        return acc

    part = lax.fori_loop(0, planes, gram_part, jnp.zeros((total_orbs + count, total_orbs), f32))
    half = (total_orbs + count) // 2
    packed = jnp.concatenate([part[:half], part[half:]], axis=1)
    copies = reduce_start(gram_slots, 0, packed)
    packed = reduce_end(gram_slots, copies, 0) * (1.0 / cells)
    full = jnp.concatenate([packed[:, :total_orbs], packed[:, total_orbs:]], axis=0)
    gram_inverse = split(inverse(full[:total_orbs]))

    def solve(correlation):
        return split(dot3(split(correlation), gram_inverse, NN))

    zero_field = jnp.zeros((count, width), f32)
    zero_inner = jnp.zeros((count, atoms), f32)
    energy = en_ref[...]
    coupling = coup_ref[...]
    freq_square = freq_ref[0] * freq_ref[0]

    g = solve(full[total_orbs:])

    def first_residual(z, carry):
        inner, norm = carry
        for y in range(rows):
            source = dv_ref[z, pl.ds(y, 1), :] * orb_ref[z, y]
            r = dot3(g, phi(z, y), NN) - source
            pad0[z + 1, y + 1] = r
            inner = inner + dot3(split(r), u(z, y), NT)
            norm = norm + r * r
        return inner, norm

    inner, norm = lax.fori_loop(0, planes, first_residual, (zero_inner, zero_field))
    halos = halo_start(pad0, 0)
    copies = reduce_start(red_slots.at[0], 1, inner)
    norm0_part = jnp.sum(norm, axis=1, keepdims=True)

    def shifted(pad, coefficients, z, y):
        centre = pad[z + 1, y + 1]
        beside = pad[z, y + 1] + pad[z + 2, y + 1] + pad[z + 1, y] + pad[z + 1, y + 2]
        beside = beside + pltpu.roll(centre, 1, 1) + pltpu.roll(centre, width - 1, 1)
        diagonal = (6.0 * kinetic_scale + vloc_ref[z, pl.ds(y, 1), :]) - energy
        return diagonal * centre - kinetic_scale * beside + dot3(coefficients, u(z, y), NN)

    inner = reduce_end(red_slots.at[0], copies, 1)
    coefficients0 = split(inner * coupling)
    for copy in halos:
        copy.wait_recv()

    def first_apply(z, carry):
        inner, norm = carry
        for y in range(rows):
            first = shifted(pad0, coefficients0, z, y)
            pad1[z + 1, y + 1] = first
            inner = inner + dot3(split(first), u(z, y), NT)
            norm = norm + first * first
        return inner, norm

    inner, norm = lax.fori_loop(0, planes, first_apply, (zero_inner, zero_field))
    halos = halo_start(pad1, 1)
    copies = reduce_start(red_slots.at[1], 2, inner)
    first0_part = jnp.sum(norm, axis=1, keepdims=True)
    inner = reduce_end(red_slots.at[1], copies, 2)
    coefficients1 = split(inner * coupling)
    for copy in halos:
        copy.wait_recv()

    def second_apply(z, correlation):
        for y in range(rows):
            target = shifted(pad1, coefficients1, z, y) + freq_square * pad0[z + 1, y + 1]
            work[z, y] = target
            correlation = correlation + dot3(split(target), phi(z, y), NT)
        return correlation

    correlation = lax.fori_loop(
        0, planes, second_apply, jnp.zeros((count, total_orbs), f32)
    )
    lane = lax.broadcasted_iota(jnp.int32, (count, atoms), 1)

    def scalars(parts):
        out = jnp.zeros((count, atoms), f32)
        for k, part in enumerate(parts):
            out = jnp.where(lane == k, part, out)
        return out

    tail = scalars((norm0_part, first0_part))[:, : red_slots.shape[3] - total_orbs]
    copies = reduce_start(red_slots.at[2], 3, jnp.concatenate([correlation, tail], axis=1))
    total = reduce_end(red_slots.at[2], copies, 3)
    norm0 = total[:, total_orbs : total_orbs + 1]
    first0 = total[:, total_orbs + 1 : total_orbs + 2]
    step0 = norm0 / (first0 + freq_square * norm0)
    g = solve(total[:, :total_orbs] * (1.0 / cells))

    def second_residual(z, carry):
        inner, norm, cross = carry
        for y in range(rows):
            before = pad0[z + 1, y + 1]
            image = work[z, y] - dot3(g, phi(z, y), NN)
            r = before - step0 * image
            pad2[z + 1, y + 1] = r
            inner = inner + dot3(split(r), u(z, y), NT)
            norm = norm + r * r
            cross = cross + r * before
        return inner, norm, cross

    inner, norm, cross = lax.fori_loop(
        0, planes, second_residual, (zero_inner, zero_field, zero_field)
    )
    halos = halo_start(pad2, 2)
    copies = reduce_start(red_slots.at[3], 4, inner)
    norm1_part = jnp.sum(norm, axis=1, keepdims=True)
    cross_part = jnp.sum(cross, axis=1, keepdims=True)
    inner = reduce_end(red_slots.at[3], copies, 4)
    coefficients2 = split(inner * coupling)
    for copy in halos:
        copy.wait_recv()

    def third_apply(z, carry):
        square, cross = carry
        for y in range(rows):
            first = shifted(pad2, coefficients2, z, y)
            work[z, y] = first
            square = square + first * first
            cross = cross + first * pad1[z + 1, y + 1]
        return square, cross

    square, cross = lax.fori_loop(0, planes, third_apply, (zero_field, zero_field))
    square_part = jnp.sum(square, axis=1, keepdims=True)
    mixed_part = jnp.sum(cross, axis=1, keepdims=True)
    copies = reduce_start(
        red_slots.at[4], 5, scalars((norm1_part, cross_part, square_part, mixed_part))
    )
    total = reduce_end(red_slots.at[4], copies, 5)
    norm1, cross, square, mixed = (total[:, k : k + 1] for k in range(4))
    ratio = norm1 / norm0
    curvature = (
        square + 2.0 * ratio * mixed + ratio * ratio * first0
        + freq_square * (norm1 + 2.0 * ratio * cross + ratio * ratio * norm0)
    )
    step1 = norm1 / curvature
    scale0 = step0 + step1 * ratio

    def finish(z, carry):
        for y in range(rows):
            response = scale0 * pad1[z + 1, y + 1] + step1 * work[z, y]
            resp_ref[z, y] = response
            dens_slots[0, z, pl.ds(y, 1), :] = jnp.sum(
                orb_ref[z, y] * response, axis=0, keepdims=True
            )
        return carry

    lax.fori_loop(0, planes, finish, 0)
    last = [
        start(dens_slots.at[0], dens_slots.at[k], dens_send.at[k - 1], dens_recv.at[k - 1],
              {"orb": lax.rem(orb + k, orbs)})
        for k in range(1, orbs)
    ]
    for copy in last:
        copy.wait_recv()
    density = dens_slots[0]
    for k in range(1, orbs):
        density = density + dens_slots[k]
    dens_ref[...] = density * (4.0 / total_orbs)
    for copy in sent:
        copy.wait_send()


def solution(mesh):
    slabs, pens, orbs = mesh.shape["slab"], mesh.shape["pen"], mesh.shape["orb"]

    def on_device(
        orbitals, energies, frequency, local_potential, perturbation, projectors, profiles,
        couplings, atom_planes,
    ):
        count, planes, rows, width = orbitals.shape
        atoms = projectors.shape[0]
        total_orbs, group = count * orbs, slabs * pens
        table = jnp.concatenate([profiles, atom_planes[:, None].astype(f32)], axis=1)
        vmem = pl.BlockSpec(memory_space=pltpu.VMEM)
        smem = pl.BlockSpec(memory_space=pltpu.SMEM)
        dma = pltpu.SemaphoreType.DMA
        response, density = pl.pallas_call(
            functools.partial(kernel, slabs, pens, orbs),
            out_shape=(
                jax.ShapeDtypeStruct((planes, rows, count, width), f32),
                jax.ShapeDtypeStruct((planes, rows, width), f32),
            ),
            in_specs=[vmem, vmem, smem, vmem, vmem, vmem, vmem, vmem],
            out_specs=(vmem, vmem),
            scratch_shapes=[
                pltpu.VMEM((orbs - 1, planes, rows, count, width), f32),
                pltpu.VMEM((planes, rows, total_orbs, width), bf16),
                pltpu.VMEM((planes, rows, total_orbs, width), bf16),
                pltpu.VMEM((planes, rows, atoms, width), bf16),
                pltpu.VMEM((planes, rows, atoms, width), bf16),
                pltpu.VMEM((planes + 2, rows + 2, count, width), f32),
                pltpu.VMEM((planes + 2, rows + 2, count, width), f32),
                pltpu.VMEM((planes + 2, rows + 2, count, width), f32),
                pltpu.VMEM((planes, rows, count, width), f32),
                pltpu.VMEM((orbs, planes, rows, width), f32),
                pltpu.VMEM((group, (total_orbs + count) // 2, 2 * total_orbs), f32),
                pltpu.VMEM((5, group, count, atoms), f32),
                dma((orbs - 1,)), dma((orbs - 1,)),
                dma((3, 4)), dma((3, 4)),
                dma((6, group - 1)), dma((6, group - 1)),
                dma((orbs - 1,)), dma((orbs - 1,)),
            ],
            compiler_params=pltpu.CompilerParams(collective_id=0, has_side_effects=True),
        )(
            jnp.transpose(orbitals, (1, 2, 0, 3)),
            energies[:, None],
            frequency,
            local_potential,
            perturbation,
            jnp.transpose(projectors, (1, 0, 2)),
            table,
            couplings[None, :],
        )
        return jnp.transpose(response, (2, 0, 1, 3)), density

    in_specs = (
        P(("parts", "orb"), "slab", "pen", None), P(("parts", "orb")), P("parts"),
        P("slab", "pen", None), P("slab", "pen", None), P(None, "pen", None), P(), P(), P(),
    )
    out_specs = (P(("parts", "orb"), "slab", "pen", None), P(("parts", "slab"), "pen", None))
    return jax.shard_map(
        on_device, mesh=mesh, in_specs=in_specs, out_specs=out_specs, check_vma=False
    )
```

time: 373 us -> 96.7 us (0.26)
  blocking collectives: 245 us -> 0 us
  Pallas kernels: 0 us -> 86.6 us
  waiting for transfers between devices: 26.6 us -> 0 us
  matrix products: 25.8 us -> 0 us
  starting transfers between devices: 17.6 us -> 0 us
  other arithmetic: 17.1 us -> 0.01 us
  local copies, waits for them, and re-layouts: 24.9 us -> 8.59 us
  between operations: 15.3 us -> 1.33 us
    psum x11 -> x0, blocking collectives: 245 us -> none  [the longest x4 104 us: coefficients(): summed = lax.psum(partial_sum, ('slab', 'pen'))]
    pallas_call x0 -> x1, Pallas kernels: none -> 86.6 us  [on_device(): pl.pallas_call(functools.partial(kernel, slabs, pens, orbs), out_shape=(j...]
    dot_general x17 -> x0, matrix products: 24.6 us -> none  [the longest x4 8.76 us: apply_section(): lax.dot_general(flat_spread, flat_beta, (((0,), (0,)), ((), ())), precisi...]
    all_gather x1 -> x0, waiting for transfers between devices: 21.8 us -> none  [on_device(): everyone = lax.all_gather(orbitals, 'orb', axis=0, tiled=True)]
    ppermute x16 -> x0, starting transfers between devices: 17.6 us -> none  [the longest x8 15.6 us: extended(): lax.ppermute(head, axis, [((i + 1) % count, i) for i in range(count)])]
    another operation x5 -> x0, other arithmetic: 12.1 us -> none  [the longest x3 6.52 us: on_device(): factor = jnp.linalg.cholesky(gram_total / cell_total)]
    slice x12 -> x0, local copies, waits for them, and re-layouts: 10 us -> none  [the longest x8 7.01 us: apply_section(): beside_all = beside_all + jnp.roll(centre, 1, 3) + jnp.roll(centre, -1, 3)]
    ppermute x16 -> x0, waiting for transfers between devices: 4.81 us -> none  [the longest x8 3.68 us: extended(): lax.ppermute(head, axis, [((i + 1) % count, i) for i in range(count)])]
  transfers between devices with their start and end apart: 17 -> 0, of which waited for: 9 -> 0; matrix products, arithmetic and copies ran while one was open for 1% -> 0% of each run, Pallas kernels for 0% -> 0%
where the time goes in v1:
time: 96.7 us; the launch traced here: 96.5 us
  Pallas kernels  86.6 us (90%)
  local copies, waits for them, and re-layouts  8.59 us (9%)
  between operations  1.33 us (1%)
    pallas_call x1, Pallas kernels, on_device(): pl.pallas_call(functools.partial(kernel, slabs, pens, orbs), out_shape=(j...  86.6 us
    unnamed x14, local copies, waits for them, and re-layouts  7.17 us

profile of v1, /device:TPU:0, one launch (start us, length us, event | category | flops | bytes accessed | tf_op | source)
XLA Modules:
  0.0 96.5 jit_solution(1273226988383720173)
XLA Ops:
  0.6 0.0 copy-start.2
  1.3 0.0 copy-start.4
  1.3 0.6 copy-done.4
  2.0 0.0 copy-done.2
  2.0 0.0 copy-start.3
  2.0 0.6 copy-done.3
  2.6 0.7 copy.19.en_ref
  3.3 0.7 copy.20.table_ref
  4.0 0.0 copy-start
  4.0 2.2 %copy.25 = f32[32,4,4,256]{3,0,2,1:T(8,128)} copy(f32[32,4,4,256]{3,2,1,0:T(4,128)} %param.9) | data formatting | bytes 1048576 | tf_op args[0]
  6.2 0.0 copy-done
  6.2 0.9 copy.24
  7.1 86.6 %shard_map.104 = (f32[4,4,32,256]{3,2,1,0:T(8,128)}, f32[4,4,256]{2,1,0:T(4,128)}) custom-call(f32[4,4,32,256]{3,2,1,0:T(8,128)} %bitcast.11, f32[32,1]{1,0:T(8,128)} %copy.19.en_ref, f32[1]{0:T(128)S(6)} %copy.27.freq_ref, f32[4,4,256]{2,1,0:T(4,128)} %vloc_ref.1, f32[4,4,256]{2,1,0:T(4,128)} %dv_ref.1, f32[4,128,256]{2,1,0:T(8,128)} %bitcast.12, ...), custom_call_target="tpu_custom_call" | custom-call | tf_op jit(solution)/shard_map/pallas_call | solution.py:347
  93.7 0.0 copy-start.1
  93.7 2.2 %copy.21 = f32[32,4,4,256]{3,2,1,0:T(4,128)} copy(f32[32,4,4,256]{3,0,2,1:T(8,128)} %bitcast.13) | data formatting | bytes 1048576
  95.9 0.0 copy-done.1
  95.9 0.6 copy.28
  (2 shorter events, 0.0 us)
Async XLA Ops:
  0.6 1.3 %copy-start.2 = (f32[128,5]{0,1:T(8,128)S(1)}, f32[128,5]{0,1:T(8,128)}, u32[]{:S(2)}) copy-start(f32[128,5]{0,1:T(8,128)} %param.15) | copy-start | bytes 7684
  1.3 0.7 copy-start.4
  2.0 0.7 copy-start.3
  4.0 2.2 %copy-start = (f32[128,4,256]{2,1,0:T(4,128)S(1)}, f32[128,4,256]{2,1,0:T(4,128)}, u32[]{:S(2)}) copy-start(f32[128,4,256]{2,1,0:T(4,128)} %param.14) | copy-start | bytes 1572868
  93.7 2.2 %copy-start.1 = (f32[4,4,256]{2,1,0:T(4,128)S(1)}, f32[4,4,256]{2,1,0:T(4,128)}, u32[]{:S(2)}) copy-start(f32[4,4,256]{2,1,0:T(4,128)} %get-tuple-element.13) | copy-start | bytes 49156

commit v2 on v1

--- a/solution.py
+++ b/solution.py
@@ -43,9 +43,9 @@
 def kernel(
     slabs, pens, orbs, orb_ref, en_ref, freq_ref, vloc_ref, dv_ref, beta_ref, table_ref, coup_ref,
     resp_ref, dens_ref,
-    others, phi_hi, phi_lo, u_hi, u_lo, pad0, pad1, pad2, work, dens_slots,
+    others, phz, phz_hi, phz_lo, dvz, tz, phi_hi, phi_lo, u_hi, u_lo, pad0, pad1, pad2, work, dens_slots,
     gram_slots, red_slots,
-    gather_send, gather_recv, halo_send, halo_recv, red_send, red_recv, dens_send, dens_recv,
+    gather_send, gather_recv, plane_send, plane_recv, halo_send, halo_recv, red_send, red_recv, dens_send, dens_recv,
 ):
     planes, rows, count, width = orb_ref.shape
     atoms = beta_ref.shape[1]
@@ -81,14 +81,33 @@
         sent.append(copy)
         return copy
 
+    pieces = [pl.ds(0, 1), pl.ds(planes - 1, 1)]
+    if planes > 2:
+        pieces.append(pl.ds(1, planes - 2))
     gathers = [
-        start(orb_ref, others.at[k - 1], gather_send.at[k - 1], gather_recv.at[k - 1],
-              {"orb": lax.rem(orb + k, orbs)})
-        for k in range(1, orbs)
+        [
+            start(orb_ref.at[piece], others.at[k - 1, piece], gather_send.at[k - 1, n],
+                  gather_recv.at[k - 1, n], {"orb": lax.rem(orb + k, orbs)})
+            for k in range(1, orbs)
+        ]
+        for n, piece in enumerate(pieces)
     ]
 
-    def halo_start(pad, index):
-        up, down = lax.rem(slab + 1, slabs), lax.rem(slab + slabs - 1, slabs)
+    up, down = lax.rem(slab + 1, slabs), lax.rem(slab + slabs - 1, slabs)
+
+    def plane_start(low, high, below, above, index):
+        return [
+            start(low, above, plane_send.at[index, 0], plane_recv.at[index, 0], {"slab": down}),
+            start(high, below, plane_send.at[index, 1], plane_recv.at[index, 1], {"slab": up}),
+        ]
+
+    beside = plane_start(
+        dv_ref.at[0], dv_ref.at[planes - 1], dvz.at[0], dvz.at[1], orbs
+    ) + plane_start(
+        orb_ref.at[0], orb_ref.at[planes - 1], phz.at[0, 0], phz.at[1, 0], 0
+    )
+
+    def halo_start(pad, index, wanted):
         right, left = lax.rem(pen + 1, pens), lax.rem(pen + pens - 1, pens)
         inner_p, inner_r = pl.ds(1, planes), pl.ds(1, rows)
         sides = (
@@ -100,6 +119,7 @@
         return [
             start(src, dst, halo_send.at[index, side], halo_recv.at[index, side], device)
             for side, (src, dst, device) in enumerate(sides)
+            if side in wanted
         ]
 
     def reduce_start(slots, index, values):
@@ -136,8 +156,16 @@
             u_hi[z, y] = hi
             u_lo[z, y] = lo
 
-    for copy in gathers:
-        copy.wait_recv()
+    for piece in gathers[:2]:
+        for copy in piece:
+            copy.wait_recv()
+    for k in range(1, orbs):
+        beside += plane_start(
+            others.at[k - 1, 0], others.at[k - 1, planes - 1], phz.at[0, k], phz.at[1, k], k
+        )
+    for piece in gathers[2:]:
+        for copy in piece:
+            copy.wait_recv()
 
     def put_phi(z, carry):
         for y in range(rows):
@@ -196,9 +224,23 @@
         return inner, norm
 
     inner, norm = lax.fori_loop(0, planes, first_residual, (zero_inner, zero_field))
-    halos = halo_start(pad0, 0)
+    halos = halo_start(pad0, 0, (2, 3))
     copies = reduce_start(red_slots.at[0], 1, inner)
     norm0_part = jnp.sum(norm, axis=1, keepdims=True)
+    for copy in beside:
+        copy.wait_recv()
+
+    def phi_beside(side, y):
+        return phz_hi[side, y], phz_lo[side, y]
+
+    for side, at in ((0, 0), (1, planes + 1)):
+        for y in range(rows):
+            for k in range(orbs):
+                hi, lo = split(phz[side, k, y])
+                phz_hi[side, y, k * count : (k + 1) * count] = hi
+                phz_lo[side, y, k * count : (k + 1) * count] = lo
+            source = dvz[side, y : y + 1, :] * phz[side, 0, y]
+            pad0[at, y + 1] = dot3(g, phi_beside(side, y), NN) - source
 
     def shifted(pad, coefficients, z, y):
         centre = pad[z + 1, y + 1]
@@ -221,13 +263,15 @@
             norm = norm + first * first
         return inner, norm
 
-    inner, norm = lax.fori_loop(0, planes, first_apply, (zero_inner, zero_field))
-    halos = halo_start(pad1, 1)
+    carry = first_apply(planes - 1, first_apply(0, (zero_inner, zero_field)))
+    halos = halo_start(pad1, 1, (0, 1))
+    inner, norm = lax.fori_loop(1, planes - 1, first_apply, carry)
+    halos += halo_start(pad1, 1, (2, 3))
     copies = reduce_start(red_slots.at[1], 2, inner)
     first0_part = jnp.sum(norm, axis=1, keepdims=True)
     inner = reduce_end(red_slots.at[1], copies, 2)
     coefficients1 = split(inner * coupling)
-    for copy in halos:
+    for copy in halos[2:]:
         copy.wait_recv()
 
     def second_apply(z, correlation):
@@ -238,8 +282,12 @@
         return correlation
 
     correlation = lax.fori_loop(
-        0, planes, second_apply, jnp.zeros((count, total_orbs), f32)
-    )
+        1, planes - 1, second_apply, jnp.zeros((count, total_orbs), f32)
+    )
+    for copy in halos[:2]:
+        copy.wait_recv()
+    correlation = second_apply(planes - 1, second_apply(0, correlation))
+    outer = plane_start(work.at[0], work.at[planes - 1], tz.at[0], tz.at[1], orbs + 1)
     lane = lax.broadcasted_iota(jnp.int32, (count, atoms), 1)
 
     def scalars(parts):
@@ -271,10 +319,16 @@
     inner, norm, cross = lax.fori_loop(
         0, planes, second_residual, (zero_inner, zero_field, zero_field)
     )
-    halos = halo_start(pad2, 2)
+    halos = halo_start(pad2, 2, (2, 3))
     copies = reduce_start(red_slots.at[3], 4, inner)
     norm1_part = jnp.sum(norm, axis=1, keepdims=True)
     cross_part = jnp.sum(cross, axis=1, keepdims=True)
+    for copy in outer:
+        copy.wait_recv()
+    for side, at in ((0, 0), (1, planes + 1)):
+        for y in range(rows):
+            image = tz[side, y] - dot3(g, phi_beside(side, y), NN)
+            pad2[at, y + 1] = pad0[at, y + 1] - step0 * image
     inner = reduce_end(red_slots.at[3], copies, 4)
     coefficients2 = split(inner * coupling)
     for copy in halos:
@@ -284,7 +338,7 @@
         square, cross = carry
         for y in range(rows):
             first = shifted(pad2, coefficients2, z, y)
-            work[z, y] = first
+            resp_ref[z, y] = first
             square = square + first * first
             cross = cross + first * pad1[z + 1, y + 1]
         return square, cross
@@ -307,7 +361,7 @@
 
     def finish(z, carry):
         for y in range(rows):
-            response = scale0 * pad1[z + 1, y + 1] + step1 * work[z, y]
+            response = scale0 * pad1[z + 1, y + 1] + step1 * resp_ref[z, y]
             resp_ref[z, y] = response
             dens_slots[0, z, pl.ds(y, 1), :] = jnp.sum(
                 orb_ref[z, y] * response, axis=0, keepdims=True
@@ -354,6 +408,11 @@
             out_specs=(vmem, vmem),
             scratch_shapes=[
                 pltpu.VMEM((orbs - 1, planes, rows, count, width), f32),
+                pltpu.VMEM((2, orbs, rows, count, width), f32),
+                pltpu.VMEM((2, rows, total_orbs, width), bf16),
+                pltpu.VMEM((2, rows, total_orbs, width), bf16),
+                pltpu.VMEM((2, rows, width), f32),
+                pltpu.VMEM((2, rows, count, width), f32),
                 pltpu.VMEM((planes, rows, total_orbs, width), bf16),
                 pltpu.VMEM((planes, rows, total_orbs, width), bf16),
                 pltpu.VMEM((planes, rows, atoms, width), bf16),
@@ -365,7 +424,8 @@
                 pltpu.VMEM((orbs, planes, rows, width), f32),
                 pltpu.VMEM((group, (total_orbs + count) // 2, 2 * total_orbs), f32),
                 pltpu.VMEM((5, group, count, atoms), f32),
-                dma((orbs - 1,)), dma((orbs - 1,)),
+                dma((orbs - 1, 3)), dma((orbs - 1, 3)),
+                dma((orbs + 2, 2)), dma((orbs + 2, 2)),
                 dma((3, 4)), dma((3, 4)),
                 dma((6, group - 1)), dma((6, group - 1)),
                 dma((orbs - 1,)), dma((orbs - 1,)),

time: 96.7 us -> 89.2 us (0.922)
  Pallas kernels: 86.6 us -> 79.1 us
    pallas_call x1, Pallas kernels: 86.6 us -> 79.1 us  [on_device(): pl.pallas_call(functools.partial(kernel, slabs, pens, orbs), out_shape=(j...]
where the time goes in v2:
time: 89.2 us; the launch traced here: 89 us
  Pallas kernels  79.1 us (89%)
  local copies, waits for them, and re-layouts  8.59 us (10%)
  between operations  1.33 us (1%)
    pallas_call x1, Pallas kernels, on_device(): pl.pallas_call(functools.partial(kernel, slabs, pens, orbs), out_shape=(j...  79.1 us
    unnamed x14, local copies, waits for them, and re-layouts  7.17 us

profile of v2, /device:TPU:0, one launch (start us, length us, event | category | flops | bytes accessed | tf_op | source)
XLA Modules:
  0.0 89.0 jit_solution(11635743241652763944)
XLA Ops:
  0.6 0.0 copy-start.2
  1.3 0.0 copy-start.4
  1.3 0.6 copy-done.4
  2.0 0.0 copy-done.2
  2.0 0.0 copy-start.3
  2.0 0.6 copy-done.3
  2.6 0.7 copy.19.en_ref
  3.3 0.7 copy.20.table_ref
  4.0 0.0 copy-start
  4.0 2.2 %copy.25 = f32[32,4,4,256]{3,0,2,1:T(8,128)} copy(f32[32,4,4,256]{3,2,1,0:T(4,128)} %param.9) | data formatting | bytes 1048576 | tf_op args[0]
  6.2 0.0 copy-done
  6.2 0.9 copy.24
  7.1 79.1 %shard_map.104 = (f32[4,4,32,256]{3,2,1,0:T(8,128)}, f32[4,4,256]{2,1,0:T(4,128)}) custom-call(f32[4,4,32,256]{3,2,1,0:T(8,128)} %bitcast.11, f32[32,1]{1,0:T(8,128)} %copy.19.en_ref, f32[1]{0:T(128)S(6)} %copy.27.freq_ref, f32[4,4,256]{2,1,0:T(4,128)} %vloc_ref.1, f32[4,4,256]{2,1,0:T(4,128)} %dv_ref.1, f32[4,128,256]{2,1,0:T(8,128)} %bitcast.12, ...), custom_call_target="tpu_custom_call" | custom-call | tf_op jit(solution)/shard_map/pallas_call | solution.py:401
  86.2 0.0 copy-start.1
  86.2 2.2 %copy.21 = f32[32,4,4,256]{3,2,1,0:T(4,128)} copy(f32[32,4,4,256]{3,0,2,1:T(8,128)} %bitcast.13) | data formatting | bytes 1048576
  88.4 0.0 copy-done.1
  88.4 0.6 copy.28
  (2 shorter events, 0.0 us)
Async XLA Ops:
  0.6 1.3 %copy-start.2 = (f32[128,5]{0,1:T(8,128)S(1)}, f32[128,5]{0,1:T(8,128)}, u32[]{:S(2)}) copy-start(f32[128,5]{0,1:T(8,128)} %param.15) | copy-start | bytes 7684
  1.3 0.7 copy-start.4
  2.0 0.7 copy-start.3
  4.0 2.2 %copy-start = (f32[128,4,256]{2,1,0:T(4,128)S(1)}, f32[128,4,256]{2,1,0:T(4,128)}, u32[]{:S(2)}) copy-start(f32[128,4,256]{2,1,0:T(4,128)} %param.14) | copy-start | bytes 1572868
  86.2 2.2 %copy-start.1 = (f32[4,4,256]{2,1,0:T(4,128)S(1)}, f32[4,4,256]{2,1,0:T(4,128)}, u32[]{:S(2)}) copy-start(f32[4,4,256]{2,1,0:T(4,128)} %get-tuple-element.13) | copy-start | bytes 49156

commit v3 on v2

--- a/solution.py
+++ b/solution.py
@@ -30,26 +30,36 @@
     size = a.shape[0]
     row_id = lax.broadcasted_iota(jnp.int32, (size, size), 0)
     col_id = lax.broadcasted_iota(jnp.int32, (size, size), 1)
-    one_row = lax.broadcasted_iota(jnp.int32, (1, size), 1)
-    for k in range(size):
-        inv = 1.0 / a[k : k + 1, k : k + 1]
-        column = a[:, k : k + 1]
-        row = jnp.where(one_row == k, inv, a[k : k + 1, :] * inv)
-        updated = jnp.where(col_id == k, 0.0, a) - column * row
-        a = jnp.where(row_id == k, row, updated)
-    return a
+    lane = lax.broadcasted_iota(jnp.int32, (1, size), 1)
+    diagonal = jnp.where(row_id == col_id, a, 0.0)
+    scale = (1.0 / jnp.sqrt(jnp.sum(diagonal, axis=1, keepdims=True))) * (
+        1.0 / jnp.sqrt(jnp.sum(diagonal, axis=0, keepdims=True))
+    )
+    a = a * scale
+    for k in range(0, size, 2):
+        p, q = a[k : k + 1, k : k + 1], a[k : k + 1, k + 1 : k + 2]
+        r, t = a[k + 1 : k + 2, k : k + 1], a[k + 1 : k + 2, k + 1 : k + 2]
+        top, low = a[k : k + 1, :], a[k + 1 : k + 2, :]
+        first, second = a[:, k : k + 1], a[:, k + 1 : k + 2]
+        inv = 1.0 / (p * t - q * r)
+        new_top = jnp.where(lane == k, t, jnp.where(lane == k + 1, -q, t * top - q * low)) * inv
+        new_low = jnp.where(lane == k, -r, jnp.where(lane == k + 1, p, p * low - r * top)) * inv
+        rest = jnp.where((col_id == k) | (col_id == k + 1), 0.0, a)
+        rest = rest - first * new_top - second * new_low
+        a = jnp.where(row_id == k, new_top, jnp.where(row_id == k + 1, new_low, rest))
+    return a * scale
 
 
 def kernel(
-    slabs, pens, orbs, orb_ref, en_ref, freq_ref, vloc_ref, dv_ref, beta_ref, table_ref, coup_ref,
+    slabs, pens, orbs, orb_ref, en_ref, freq_ref, vloc_ref, dv_ref, beta_ref, prof_ref, atom_ref, coup_ref,
     resp_ref, dens_ref,
     others, phz, phz_hi, phz_lo, dvz, tz, phi_hi, phi_lo, u_hi, u_lo, pad0, pad1, pad2, work, dens_slots,
     gram_slots, red_slots,
     gather_send, gather_recv, plane_send, plane_recv, halo_send, halo_recv, red_send, red_recv, dens_send, dens_recv,
 ):
     planes, rows, count, width = orb_ref.shape
-    atoms = beta_ref.shape[1]
-    span = table_ref.shape[1] - 1
+    atoms = beta_ref.shape[0]
+    span = prof_ref.shape[0]
     total_orbs = count * orbs
     depth = planes * slabs
     cells = float(depth * rows * pens * width)
@@ -143,16 +153,23 @@
             total = total + slots[k]
         return total
 
-    atom = table_ref[:, span : span + 1]
+    def as_column(row):
+        size = row.shape[1]
+        row_id = lax.broadcasted_iota(jnp.int32, (size, size), 0)
+        col_id = lax.broadcasted_iota(jnp.int32, (size, size), 1)
+        return jnp.sum(jnp.where(row_id == col_id, row, 0.0), axis=1, keepdims=True)
+
+    atom = atom_ref[...]
     for z in range(planes):
-        plane = (slab * planes + z).astype(f32)
-        weight = jnp.zeros((atoms, 1), f32)
+        plane = slab * planes + z
+        weight = jnp.zeros((1, atoms), f32)
         for d in range(span):
-            covered = atom + float(d)
-            covered = jnp.where(covered >= float(depth), covered - float(depth), covered)
-            weight = weight + jnp.where(covered == plane, table_ref[:, d : d + 1], 0.0)
-        for y in range(rows):
-            hi, lo = split(beta_ref[y] * weight)
+            covered = atom + d
+            covered = jnp.where(covered >= depth, covered - depth, covered)
+            weight = weight + jnp.where(covered == plane, prof_ref[d : d + 1, :], 0.0)
+        weight = as_column(weight)
+        for y in range(rows):
+            hi, lo = split(beta_ref[:, y, :] * weight)
             u_hi[z, y] = hi
             u_lo[z, y] = lo
 
@@ -207,7 +224,7 @@
 
     zero_field = jnp.zeros((count, width), f32)
     zero_inner = jnp.zeros((count, atoms), f32)
-    energy = en_ref[...]
+    energy = as_column(en_ref[...])
     coupling = coup_ref[...]
     freq_square = freq_ref[0] * freq_ref[0]
 
@@ -394,7 +411,6 @@
         count, planes, rows, width = orbitals.shape
         atoms = projectors.shape[0]
         total_orbs, group = count * orbs, slabs * pens
-        table = jnp.concatenate([profiles, atom_planes[:, None].astype(f32)], axis=1)
         vmem = pl.BlockSpec(memory_space=pltpu.VMEM)
         smem = pl.BlockSpec(memory_space=pltpu.SMEM)
         dma = pltpu.SemaphoreType.DMA
@@ -404,7 +420,7 @@
                 jax.ShapeDtypeStruct((planes, rows, count, width), f32),
                 jax.ShapeDtypeStruct((planes, rows, width), f32),
             ),
-            in_specs=[vmem, vmem, smem, vmem, vmem, vmem, vmem, vmem],
+            in_specs=[vmem, vmem, smem, vmem, vmem, vmem, vmem, vmem, vmem],
             out_specs=(vmem, vmem),
             scratch_shapes=[
                 pltpu.VMEM((orbs - 1, planes, rows, count, width), f32),
@@ -433,12 +449,13 @@
             compiler_params=pltpu.CompilerParams(collective_id=0, has_side_effects=True),
         )(
             jnp.transpose(orbitals, (1, 2, 0, 3)),
-            energies[:, None],
+            energies[None, :],
             frequency,
             local_potential,
             perturbation,
-            jnp.transpose(projectors, (1, 0, 2)),
-            table,
+            projectors,
+            profiles.T,
+            atom_planes[None, :],
             couplings[None, :],
         )
         return jnp.transpose(response, (2, 0, 1, 3)), density

time: 89.2 us -> 87.3 us (0.979)
  local copies, waits for them, and re-layouts: 8.59 us -> 4.93 us
  Pallas kernels: 79.1 us -> 80.9 us
    unnamed x14 -> x5, local copies, waits for them, and re-layouts: 7.17 us -> 4.93 us
    pallas_call x1, Pallas kernels: 79.1 us -> 80.9 us  [on_device(): pl.pallas_call(functools.partial(kernel, slabs, pens, orbs), out_shape=(j...]
where the time goes in v3:
time: 87.3 us; the launch traced here: 87.1 us
  Pallas kernels  80.9 us (93%)
  local copies, waits for them, and re-layouts  4.93 us (6%)
  between operations  1.29 us (1%)
    pallas_call x1, Pallas kernels, on_device(): pl.pallas_call(functools.partial(kernel, slabs, pens, orbs), out_shape=(j...  80.9 us
    unnamed x5, local copies, waits for them, and re-layouts  4.93 us

profile of v3, /device:TPU:0, one launch (start us, length us, event | category | flops | bytes accessed | tf_op | source)
XLA Modules:
  0.0 87.1 jit_solution(8578887754087532695)
XLA Ops:
  1.3 2.1 %copy.14 = f32[32,4,4,256]{3,0,2,1:T(8,128)} copy(f32[32,4,4,256]{3,2,1,0:T(4,128)} %param.9) | data formatting | bytes 1048576 | tf_op args[0]
  3.4 80.9 %shard_map.104 = (f32[4,4,32,256]{3,2,1,0:T(8,128)}, f32[4,4,256]{2,1,0:T(4,128)}) custom-call(f32[4,4,32,256]{3,2,1,0:T(8,128)} %bitcast.8, f32[1,32]{1,0:T(1,128)} %bitcast.11, f32[1]{0:T(128)S(6)} %copy.16.freq_ref, f32[4,4,256]{2,1,0:T(4,128)} %vloc_ref.1, f32[4,4,256]{2,1,0:T(4,128)} %dv_ref.1, f32[128,4,256]{2,1,0:T(4,128)} %beta_ref.1, ...), custom_call_target="tpu_custom_call" | custom-call | tf_op jit(solution)/shard_map/pallas_call | solution.py:417
  84.3 0.0 copy-start
  84.3 2.2 %copy.12 = f32[32,4,4,256]{3,2,1,0:T(4,128)} copy(f32[32,4,4,256]{3,0,2,1:T(8,128)} %bitcast.9) | data formatting | bytes 1048576
  86.5 0.0 copy-done
  86.5 0.6 copy.17
Async XLA Ops:
  84.3 2.2 %copy-start = (f32[4,4,256]{2,1,0:T(4,128)S(1)}, f32[4,4,256]{2,1,0:T(4,128)}, u32[]{:S(2)}) copy-start(f32[4,4,256]{2,1,0:T(4,128)} %get-tuple-element.11) | copy-start | bytes 49156

commit v4 on v3

--- a/solution.py
+++ b/solution.py
@@ -48,6 +48,12 @@
         rest = rest - first * new_top - second * new_low
         a = jnp.where(row_id == k, new_top, jnp.where(row_id == k + 1, new_low, rest))
     return a * scale
+
+
+def loop(low, high, body, carry):
+    for z in range(low, high):
+        carry = body(z, carry)
+    return carry
 
 
 def kernel(
@@ -192,7 +198,7 @@
                 phi_lo[z, y, k * count : (k + 1) * count] = lo
         return carry
 
-    lax.fori_loop(0, planes, put_phi, 0)
+    loop(0, planes, put_phi, 0)
 
     def phi(z, y):
         return phi_hi[z, y], phi_lo[z, y]
@@ -211,7 +217,7 @@
             acc = acc + dot3(left, phi(z, y), NT)
         return acc
 
-    part = lax.fori_loop(0, planes, gram_part, jnp.zeros((total_orbs + count, total_orbs), f32))
+    part = loop(0, planes, gram_part, jnp.zeros((total_orbs + count, total_orbs), f32))
     half = (total_orbs + count) // 2
     packed = jnp.concatenate([part[:half], part[half:]], axis=1)
     copies = reduce_start(gram_slots, 0, packed)
@@ -240,7 +246,7 @@
             norm = norm + r * r
         return inner, norm
 
-    inner, norm = lax.fori_loop(0, planes, first_residual, (zero_inner, zero_field))
+    inner, norm = loop(0, planes, first_residual, (zero_inner, zero_field))
     halos = halo_start(pad0, 0, (2, 3))
     copies = reduce_start(red_slots.at[0], 1, inner)
     norm0_part = jnp.sum(norm, axis=1, keepdims=True)
@@ -282,7 +288,7 @@
 
     carry = first_apply(planes - 1, first_apply(0, (zero_inner, zero_field)))
     halos = halo_start(pad1, 1, (0, 1))
-    inner, norm = lax.fori_loop(1, planes - 1, first_apply, carry)
+    inner, norm = loop(1, planes - 1, first_apply, carry)
     halos += halo_start(pad1, 1, (2, 3))
     copies = reduce_start(red_slots.at[1], 2, inner)
     first0_part = jnp.sum(norm, axis=1, keepdims=True)
@@ -298,7 +304,7 @@
             correlation = correlation + dot3(split(target), phi(z, y), NT)
         return correlation
 
-    correlation = lax.fori_loop(
+    correlation = loop(
         1, planes - 1, second_apply, jnp.zeros((count, total_orbs), f32)
     )
     for copy in halos[:2]:
@@ -333,7 +339,7 @@
             cross = cross + r * before
         return inner, norm, cross
 
-    inner, norm, cross = lax.fori_loop(
+    inner, norm, cross = loop(
         0, planes, second_residual, (zero_inner, zero_field, zero_field)
     )
     halos = halo_start(pad2, 2, (2, 3))
@@ -360,7 +366,7 @@
             cross = cross + first * pad1[z + 1, y + 1]
         return square, cross
 
-    square, cross = lax.fori_loop(0, planes, third_apply, (zero_field, zero_field))
+    square, cross = loop(0, planes, third_apply, (zero_field, zero_field))
     square_part = jnp.sum(square, axis=1, keepdims=True)
     mixed_part = jnp.sum(cross, axis=1, keepdims=True)
     copies = reduce_start(
@@ -385,7 +391,7 @@
             )
         return carry
 
-    lax.fori_loop(0, planes, finish, 0)
+    loop(0, planes, finish, 0)
     last = [
         start(dens_slots.at[0], dens_slots.at[k], dens_send.at[k - 1], dens_recv.at[k - 1],
               {"orb": lax.rem(orb + k, orbs)})

time: 87.3 us -> 86 us (0.985)
  Pallas kernels: 80.9 us -> 79.6 us
    pallas_call x1, Pallas kernels: 80.9 us -> 79.6 us  [on_device(): pl.pallas_call(functools.partial(kernel, slabs, pens, orbs), out_shape=(j...]
where the time goes in v4:
time: 86 us; the launch traced here: 85.8 us
  Pallas kernels  79.6 us (93%)
  local copies, waits for them, and re-layouts  4.93 us (6%)
  between operations  1.29 us (2%)
    pallas_call x1, Pallas kernels, on_device(): pl.pallas_call(functools.partial(kernel, slabs, pens, orbs), out_shape=(j...  79.6 us
    unnamed x5, local copies, waits for them, and re-layouts  4.93 us

profile of v4, /device:TPU:0, one launch (start us, length us, event | category | flops | bytes accessed | tf_op | source)
XLA Modules:
  0.0 85.8 jit_solution(15864151966602301995)
XLA Ops:
  1.3 2.1 %copy.14 = f32[32,4,4,256]{3,0,2,1:T(8,128)} copy(f32[32,4,4,256]{3,2,1,0:T(4,128)} %param.9) | data formatting | bytes 1048576 | tf_op args[0]
  3.4 79.6 %shard_map.104 = (f32[4,4,32,256]{3,2,1,0:T(8,128)}, f32[4,4,256]{2,1,0:T(4,128)}) custom-call(f32[4,4,32,256]{3,2,1,0:T(8,128)} %bitcast.8, f32[1,32]{1,0:T(1,128)} %bitcast.11, f32[1]{0:T(128)S(6)} %copy.16.freq_ref, f32[4,4,256]{2,1,0:T(4,128)} %vloc_ref.1, f32[4,4,256]{2,1,0:T(4,128)} %dv_ref.1, f32[128,4,256]{2,1,0:T(4,128)} %beta_ref.1, ...), custom_call_target="tpu_custom_call" | custom-call | tf_op jit(solution)/shard_map/pallas_call | solution.py:423
  83.0 0.0 copy-start
  83.0 2.2 %copy.12 = f32[32,4,4,256]{3,2,1,0:T(4,128)} copy(f32[32,4,4,256]{3,0,2,1:T(8,128)} %bitcast.9) | data formatting | bytes 1048576
  85.2 0.0 copy-done
  85.2 0.6 copy.17
Async XLA Ops:
  83.0 2.2 %copy-start = (f32[4,4,256]{2,1,0:T(4,128)S(1)}, f32[4,4,256]{2,1,0:T(4,128)}, u32[]{:S(2)}) copy-start(f32[4,4,256]{2,1,0:T(4,128)} %get-tuple-element.11) | copy-start | bytes 49156
